TPU v7x, 512 devices: a whole 4x4x16 slice. The times are simulated.
512 devices in a mesh: dp: 128 (over y, z, core), tensor: 4 (over x).
Axes of the slice: x: 4, y: 4, z: 16, core: 2. Of those that a mesh axis runs over, the one named last changes fastest.
Arguments:
- acts: bfloat16 [8, 32768, 2048], P(None, 'dp', 'tensor'), may hold values from -24 to 24
- out_cot: bfloat16 [8, 32768, 1024], P(None, 'dp', 'tensor'), may hold values from -24 to 24
- emb_ids: int32 [32768], P(('dp', 'tensor')), may hold values from 0 to 8191
- emb_cot: bfloat16 [32768, 1024], P('dp', 'tensor'), may hold values from -24 to 24
- grad_w: float32 [8192, 2048], P(('dp', 'tensor')), may hold values from -6 to 6
- grad_e: float32 [8192, 1024], P(('dp', 'tensor')), may hold values from -6 to 6
Outputs:
- update_w: float32 [8192, 2048], P('dp', 'tensor')
- update_e: float32 [8192, 1024], P(('dp', 'tensor'))
All inputs are finite; a program needn't handle non-finite values. Where the computation divides by a largest or mean magnitude, that divisor is 1e-20 or more.
Results may differ from a plain program's by a relative error of at most 0.0003.
Values sent between devices are 32-bit elements; how exact they have to be, the bound alone decides.
A program may use at most 64 MiB of HBM per device.

v0:
```python
import jax
import jax.numpy as jnp
from jax import lax
from jax.sharding import PartitionSpec as P

HEAD = 64
NS_ITERS = 4
damp_root = 0.7


def newton_inverse(matrices):
    size = matrices.shape[-1]
    eye = jnp.eye(size, dtype=jnp.float32)
    bound = jnp.max(jnp.sum(jnp.abs(matrices), axis=-1), axis=-1)
    approx = eye[None] / bound[:, None, None]
    for sweep in range(NS_ITERS):
        image = jnp.einsum("bij,bjk->bik", matrices, approx, precision=lax.Precision.HIGHEST)
        approx = jnp.einsum(
            "bij,bjk->bik", approx, 2.0 * eye[None] - image, precision=lax.Precision.HIGHEST
        )
    return approx


def local(acts, out_cot, emb_ids, emb_cot, grad_w, grad_e):
    n_dp = lax.axis_size("dp")
    n_tp = lax.axis_size("tensor")
    layers, tok_rows, inner_part = acts.shape
    width_part = out_cot.shape[2]
    heads_part = inner_part // HEAD
    groups_part = width_part // HEAD
    tokens_all = tok_rows * n_dp
    width = width_part * n_tp
    inner = inner_part * n_tp
    groups_all = width // HEAD
    rows_e = grad_e.shape[0]
    vocab = rows_e * n_dp * n_tp
    dp_index = lax.axis_index("dp")
    flat_index = dp_index * n_tp + lax.axis_index("tensor")
    tile_rows = grad_w.shape[0] * n_tp
    block_rows = tile_rows // HEAD
    layer_rows = min(tile_rows, width)
    layer_span = tile_rows // layer_rows
    first_layer = dp_index * tile_rows // width
    split_acts = acts.reshape(layers, tok_rows, heads_part, HEAD)
    gram_a = jnp.einsum(
        "lthi,lthj->lhij", split_acts, split_acts, preferred_element_type=jnp.float32
    )
    split_cot = out_cot.reshape(layers, tok_rows, groups_part, HEAD)
    gram_g = jnp.einsum("lthi,lthj->lhij", split_cot, split_cot, preferred_element_type=jnp.float32)
    split_emb = emb_cot.reshape(tok_rows, groups_part, HEAD)
    gram_e = jnp.einsum("thi,thj->hij", split_emb, split_emb, preferred_element_type=jnp.float32)
    blocks = jnp.concatenate(
        [gram_a.reshape(-1, HEAD, HEAD), gram_g.reshape(-1, HEAD, HEAD), gram_e], axis=0
    )
    block_count = blocks.shape[0]
    diagonal_sums = jnp.trace(blocks, axis1=1, axis2=2)
    local_a = jnp.sum(diagonal_sums[: layers * heads_part].reshape(layers, heads_part), axis=1)
    local_g = jnp.sum(
        diagonal_sums[layers * heads_part : layers * (heads_part + groups_part)].reshape(
            layers, groups_part
        ),
        axis=1,
    )
    local_e = jnp.sum(diagonal_sums[layers * (heads_part + groups_part) :])
    trace_local = jnp.concatenate([local_a, local_g, local_e[None]])
    local_counts = jnp.sum(
        (emb_ids[:, None] == jnp.arange(vocab, dtype=jnp.int32)[None, :]).astype(jnp.float32),
        axis=0,
    )
    traces, counts_all = lax.psum((trace_local, local_counts), ("dp", "tensor"))
    counts_mine = lax.dynamic_slice_in_dim(counts_all, flat_index * rows_e, rows_e)
    trace_a = traces[:layers]
    trace_g = traces[layers : 2 * layers]
    trace_e = traces[2 * layers]
    ratio = jnp.sqrt(trace_a / (tokens_all * inner) / (trace_g / (tokens_all * width)))
    ratio_e = jnp.sqrt(tokens_all / vocab / (trace_e / (tokens_all * width)))
    shift = jnp.concatenate(
        [
            jnp.repeat(damp_root * ratio, heads_part),
            jnp.repeat(damp_root / ratio, groups_part),
            jnp.full((groups_part,), 1.0, jnp.float32) * (damp_root / ratio_e),
        ]
    )
    eye = jnp.eye(HEAD, dtype=jnp.float32)
    owned = -(-block_count // n_dp)
    slots = owned * n_dp
    padded = jnp.pad(blocks.reshape(block_count, HEAD * HEAD), ((0, slots - block_count), (0, 0)))
    mine = lax.psum_scatter(padded, "dp", scatter_dimension=0, tiled=True)
    shift_pad = jnp.pad(shift, (0, slots - block_count), constant_values=1.0)
    shift_mine = lax.dynamic_slice_in_dim(shift_pad, dp_index * owned, owned)
    damped = mine.reshape(owned, HEAD, HEAD) / tokens_all + shift_mine[:, None, None] * eye
    inverse_mine = newton_inverse(damped)
    gathered = lax.all_gather(inverse_mine.reshape(owned, HEAD * HEAD), "dp", axis=0, tiled=True)
    inverses = gathered[:block_count].reshape(block_count, HEAD, HEAD)
    inv_a = inverses[: layers * heads_part].reshape(layers, heads_part, HEAD, HEAD)
    inv_g_part = inverses[layers * heads_part : layers * (heads_part + groups_part)].reshape(
        layers, groups_part, HEAD * HEAD
    )
    inv_e_part = inverses[layers * (heads_part + groups_part) :].reshape(groups_part, HEAD * HEAD)
    base_layer = 0
    sending = jnp.concatenate(
        [inv_g_part.reshape(layers * groups_part, HEAD * HEAD), inv_e_part], axis=0
    )
    shared = lax.all_gather(sending[None], "tensor", axis=0, tiled=True)
    inv_g = shared[:, : layers * groups_part].reshape(n_tp, layers, groups_part, HEAD, HEAD)
    inv_g = jnp.transpose(inv_g, (1, 0, 2, 3, 4)).reshape(layers * groups_all, HEAD, HEAD)
    inv_e = shared[:, layers * groups_part :].reshape(groups_all, HEAD, HEAD)
    tile = lax.all_to_all(grad_w, "tensor", split_axis=1, concat_axis=0, tiled=True)
    g_sel = lax.dynamic_slice_in_dim(
        inv_g, dp_index * block_rows - base_layer * groups_all, block_rows, 0
    )
    left = jnp.einsum(
        "bij,bjc->bic",
        g_sel,
        tile.reshape(block_rows, HEAD, inner_part),
        precision=lax.Precision.HIGHEST,
    )
    a_sel = lax.dynamic_slice_in_dim(inv_a, first_layer, layer_span, 0)
    right = jnp.einsum(
        "lrhi,lhij->lrhj",
        left.reshape(layer_span, layer_rows, heads_part, HEAD),
        a_sel,
        precision=lax.Precision.HIGHEST,
    )
    update_w = right.reshape(tile_rows, inner_part)
    scaled = jnp.einsum(
        "rgi,gij->rgj",
        grad_e.reshape(rows_e, groups_all, HEAD),
        inv_e,
        precision=lax.Precision.HIGHEST,
    )
    update_e = scaled.reshape(rows_e, width) / (counts_mine + damp_root * ratio_e)[:, None]
    return (update_w, update_e)


def solution(mesh):
    in_specs = (
        P(None, "dp", "tensor"),
        P(None, "dp", "tensor"),
        P(("dp", "tensor")),
        P("dp", "tensor"),
        P(("dp", "tensor"), None),
        P(("dp", "tensor"), None),
    )
    out_specs = (P("dp", "tensor"), P(("dp", "tensor"), None))
    return jax.shard_map(local, mesh=mesh, in_specs=in_specs, out_specs=out_specs, check_vma=False)
```

profile of v0, /device:TPU:1, one launch (start us, length us, event | category | flops | bytes accessed | tf_op | source)
XLA Modules:
  0.0 588.8 jit_solution(13494018394217157497)
XLA Ops:
  7.2 3.9 copy.48
  11.1 3.0 fusion.24
  14.2 1.3 copy.49
  15.5 2.0 fusion.25
  17.8 1.6 concatenate.21
  19.4 1.1 concatenate.22
  20.7 2.9 select_maximum_fusion
  23.7 0.8 fusion
  25.0 0.7 slice_reduce_fusion.1
  25.7 0.3 convert_reduce_fusion
  26.0 0.7 pad_maximum_fusion
  26.7 112.1 %all-reduce.3 = (f32[17]{0:T(128)S(1)}, f32[8192]{0:T(1024)S(1)}) all-reduce(f32[17]{0:T(128)S(1)} %pad_maximum_fusion, f32[8192]{0:T(1024)S(1)} %convert_reduce_fusion), channel_id=1, replica_groups=mesh['dp'=128,'tensor'=4] {'dp','tensor'}, use_global_device_ids=true, to_apply=%region_5.6 | all-reduce | flops 8209 | bytes 65672 | tf_op jit(solution)/shard_map/psum | solution.py:70
  138.8 0.6 slice.50
  140.7 0.6 dynamic_slice.12
  141.2 0.7 fusion.12
  142.0 1.3 dynamic-slice
  143.3 237.0 %all-reduce.6.cloned.1.call-done = f32[128,4096]{1,0:T(8,128)} async-done(((f32[128,4096]{1,0:T(8,128)}), f32[128,4096]{1,0:T(8,128)}) %all-reduce.6.cloned.1.call-update) | async-done | bytes 2097168
  380.3 0.5 broadcast.202
  380.8 2.3 add_reduce_fusion
  383.2 0.8 abs_reduce_fusion
  384.0 0.6 reduce_max.9
  385.3 0.8 convolution_subtract_fusion.3
  386.4 0.2 convolution_subtract_fusion.2
  386.5 0.2 fusion.27
  386.7 0.2 convolution_subtract_fusion.1
  386.9 0.2 fusion.28
  387.0 0.2 convolution_subtract_fusion
  387.2 0.2 fusion.29
  387.4 0.7 reshape.283
  388.1 139.9 %all-gather.6.cloned.1.call-done = f32[128,1,4096]{2,1,0:T(1,128)} async-done(((f32[1,1,4096]{2,1,0:T(1,128)}), f32[128,1,4096]{2,1,0:T(1,128)}) %all-gather.6.cloned.1.call-update) | async-done | bytes 2097168 | tf_op jit(solution)/shard_map/all_gather | solution.py:93
  528.0 1.3 slice_bitcast_fusion
  529.3 1.2 copy.52
  530.5 0.7 copy.64
  531.2 4.0 all-to-all-start
  535.3 4.7 all-to-all-done
  540.1 2.7 slice_reduce_fusion
  542.8 2.2 reshape.272
  545.0 24.2 %all-gather.8.cloned.1.call-done = f32[4,36,4096]{2,1,0:T(8,128)} async-done(((f32[1,36,4096]{2,1,0:T(8,128)}), f32[4,36,4096]{2,1,0:T(8,128)}) %all-gather.8.cloned.1.call-update) | async-done | bytes 2359312 | tf_op jit(solution)/shard_map/all_gather | solution.py:104
  569.1 1.1 slice.59
  570.2 0.3 reshape.279
  570.5 0.6 convolution_bitcast_fusion
  571.2 1.6 slice-done
  572.8 3.0 reshape.274
  575.8 2.5 copy.53
  578.3 0.9 fusion.8
  579.2 1.6 fusion.1
  580.8 0.8 copy.58
  581.5 0.7 broadcast_divide_fusion
  (46 shorter events, 2.4 us)
Async XLA Ops:
  7.2 373.2 %all-reduce.6.cloned.1.call-start = ((), (), s32[]{:S(2)}) async-start(), calls=%async_computation.3 | async-start | bytes 4194304
  11.1 3.0 copy-start.1
  15.5 2.0 copy-start.2
  23.6 2.1 copy-start.5
  23.6 504.4 %all-gather.6.cloned.1.call-start = ((), (), s32[]{:S(2)}) async-start(), calls=%async_computation.1 | async-start | bytes 2113536 | tf_op jit(solution)/shard_map/all_gather | solution.py:93
  142.0 388.5 %copy-start.3 = (f32[16,2048]{1,0:T(8,128)S(1)}, f32[16,2048]{1,0:T(8,128)}, u32[]{:S(2)}) copy-start(f32[16,2048]{1,0:T(8,128)} %param.10) | copy-start | bytes 393220
  386.5 148.6 %copy-start.4 = (f32[16,1024]{1,0:T(8,128)S(1)}, f32[16,1024]{1,0:T(8,128)}, u32[]{:S(2)}) copy-start(f32[16,1024]{1,0:T(8,128)} %param.11) | copy-start | bytes 196612
  388.1 181.0 %all-gather.8.cloned.1.call-start = ((), (), s32[]{:S(2)}) async-start(), calls=%async_computation.2 | async-start | bytes 3276800 | tf_op jit(solution)/shard_map/all_gather | solution.py:104
  528.0 12.1 %copy-start = (f32[128,1,4096]{2,1,0:T(1,128)S(1)}, f32[128,1,4096]{2,1,0:T(1,128)}, u32[]{:S(2)}) copy-start(f32[128,1,4096]{2,1,0:T(1,128)} %all-gather.6.cloned.1.call-done) | copy-start | bytes 6291460
  531.2 8.8 %all-to-all-start = ((f32[16,4,512]{2,0,1:T(8,128)}), f32[16,4,512]{2,0,1:T(8,128)S(1)}, u32[]{:S(2)}, u32[]{:S(2)}) async-start(f32[16,4,512]{2,0,1:T(8,128)} %bitcast.65), calls=%async_computation | async-start | bytes 262144 | tf_op jit(solution)/shard_map/all_to_all | solution.py:108
  571.2 1.6 slice-start
Sparse Core Ops, SparseCore 0:
  23.7 356.5 all-reduce.5
  388.2 139.7 all-gather.5
  530.6 38.4 all-gather.7
where the time goes:
time: 589 us
  waiting for transfers between devices  406 us (69%)
  blocking collectives  112 us (19%)
  local copies, waits for them, and re-layouts  30.4 us (5%)
  between operations  15.5 us (3%)
  other arithmetic  11 us (2%)
  matrix products  10.1 us (2%)
    unnamed x4, waiting for transfers between devices  237 us
    all_gather x1, waiting for transfers between devices, local(): lax.all_gather(inverse_mine.reshape(owned, HEAD * HEAD), 'dp', axis=0, ti...  140 us
    psum x1, blocking collectives, local(): traces, counts_all = lax.psum((trace_local, local_counts), ('dp', 'tensor'))  112 us
    all_gather x1, waiting for transfers between devices, local(): shared = lax.all_gather(sending[None], 'tensor', axis=0, tiled=True)  24.2 us
  transfers between devices with their start and end apart: 4, of which 4 were waited for; matrix products, arithmetic and copies ran while one was open for 2% of the time, Pallas kernels for 0%

commit v1 on v0

--- a/solution.py
+++ b/solution.py
@@ -90,7 +90,16 @@
     shift_mine = lax.dynamic_slice_in_dim(shift_pad, dp_index * owned, owned)
     damped = mine.reshape(owned, HEAD, HEAD) / tokens_all + shift_mine[:, None, None] * eye
     inverse_mine = newton_inverse(damped)
-    gathered = lax.all_gather(inverse_mine.reshape(owned, HEAD * HEAD), "dp", axis=0, tiled=True)
+    here_x = inverse_mine.reshape(owned, HEAD * HEAD)
+    gathered = jnp.concatenate(
+        lax.all_to_all(
+            jnp.stack([here_x] * lax.psum(1, axis_name="dp")),
+            axis_name="dp",
+            split_axis=0,
+            concat_axis=0,
+        ),
+        0,
+    )
     inverses = gathered[:block_count].reshape(block_count, HEAD, HEAD)
     inv_a = inverses[: layers * heads_part].reshape(layers, heads_part, HEAD, HEAD)
     inv_g_part = inverses[layers * heads_part : layers * (heads_part + groups_part)].reshape(

time: 589 us -> 561 us (0.952)
  waiting for transfers between devices: 406 us -> 263 us
  blocking collectives: 112 us -> 225 us
    all_gather x1 -> x0, waiting for transfers between devices: 140 us -> none  [local(): lax.all_gather(inverse_mine.reshape(owned, HEAD * HEAD), 'dp', axis=0, ti...]
    all_to_all x0 -> x1, blocking collectives: none -> 113 us  [local(): lax.all_to_all(jnp.stack([here_x] * lax.psum(1, axis_name='dp')), axis_na...]
    unnamed x4 -> x3, waiting for transfers between devices: 237 us -> 237 us
  transfers between devices with their start and end apart: 4 -> 3, of which waited for: 4 -> 3; matrix products, arithmetic and copies ran while one was open for 2% -> 2% of each run, Pallas kernels for 0% -> 0%
where the time goes in v1:
time: 561 us; the launch traced here: 560 us
  waiting for transfers between devices  263 us (47%)
  blocking collectives  225 us (40%)
  local copies, waits for them, and re-layouts  29.7 us (5%)
  between operations  15.8 us (3%)
  other arithmetic  11.9 us (2%)
  matrix products  10.1 us (2%)
    unnamed x3, waiting for transfers between devices  237 us
    all_to_all x1, blocking collectives, local(): lax.all_to_all(jnp.stack([here_x] * lax.psum(1, axis_name='dp')), axis_na...  113 us
    psum x1, blocking collectives, local(): traces, counts_all = lax.psum((trace_local, local_counts), ('dp', 'tensor'))  112 us
    all_gather x1, waiting for transfers between devices, local(): shared = lax.all_gather(sending[None], 'tensor', axis=0, tiled=True)  21.7 us
  transfers between devices with their start and end apart: 3, of which 3 were waited for; matrix products, arithmetic and copies ran while one was open for 2% of the time, Pallas kernels for 0%

profile of v1, /device:TPU:1, one launch (start us, length us, event | category | flops | bytes accessed | tf_op | source)
XLA Modules:
  0.0 559.9 jit_solution(15863594401988175615)
XLA Ops:
  7.2 3.9 copy.43
  11.1 3.0 fusion.24
  14.2 1.3 copy.44
  15.5 2.0 fusion.25
  17.8 1.6 concatenate.21
  19.4 1.1 concatenate.22
  20.7 2.9 select_maximum_fusion
  23.7 0.8 fusion
  25.0 0.7 slice_reduce_fusion.1
  25.7 0.3 convert_reduce_fusion
  26.0 0.7 pad_maximum_fusion
  26.7 112.1 %all-reduce.3 = (f32[17]{0:T(128)S(1)}, f32[8192]{0:T(1024)S(1)}) all-reduce(f32[17]{0:T(128)S(1)} %pad_maximum_fusion, f32[8192]{0:T(1024)S(1)} %convert_reduce_fusion), channel_id=1, replica_groups=mesh['dp'=128,'tensor'=4] {'dp','tensor'}, use_global_device_ids=true, to_apply=%region_5.6 | all-reduce | flops 8209 | bytes 65672 | tf_op jit(solution)/shard_map/psum | solution.py:70
  138.8 0.6 slice.54
  140.7 0.6 dynamic_slice.12
  141.2 0.7 fusion.12
  142.0 1.3 dynamic-slice
  143.3 237.1 %all-reduce.6.cloned.1.call-done = f32[128,4096]{1,0:T(8,128)} async-done(((f32[128,4096]{1,0:T(8,128)}), f32[128,4096]{1,0:T(8,128)}) %all-reduce.6.cloned.1.call-update) | async-done | bytes 2097168
  380.4 0.5 broadcast.204
  380.9 2.3 add_reduce_fusion
  383.2 0.8 abs_reduce_fusion
  384.1 0.6 reduce_max.9
  385.4 0.8 convolution_subtract_fusion.3
  386.4 0.2 convolution_subtract_fusion.2
  386.6 0.2 fusion.27
  386.8 0.2 convolution_subtract_fusion.1
  386.9 0.2 fusion.28
  387.1 0.2 convolution_subtract_fusion
  387.3 0.2 fusion.29
  387.5 2.1 stack.3
  389.6 112.9 %all_to_all.21 = f32[128,1,4096]{2,1,0:T(1,128)S(1)} all-to-all(f32[128,1,4096]{2,1,0:T(1,128)S(1)} %stack.3), channel_id=1, replica_groups=mesh['dp'=128,'tensor'=4] {'dp'}, dimensions={0} | all-to-all | bytes 4194304 | tf_op jit(solution)/shard_map/all_to_all | solution.py:95
  502.5 0.3 copy.61
  502.9 0.9 maximum_bitcast_fusion
  503.8 0.7 copy.62
  504.5 4.0 all-to-all-start.1
  508.6 4.7 all-to-all-done.1
  513.4 2.7 slice_reduce_fusion
  516.1 2.2 reshape.277
  518.3 21.7 %all-gather.4.cloned.1.call-done = f32[4,36,4096]{2,1,0:T(8,128)} async-done(((f32[1,36,4096]{2,1,0:T(8,128)}), f32[4,36,4096]{2,1,0:T(8,128)}) %all-gather.4.cloned.1.call-update) | async-done | bytes 2359312 | tf_op jit(solution)/shard_map/all_gather | solution.py:113
  540.0 1.1 slice.64
  541.0 0.3 reshape.285
  541.3 0.6 convolution_bitcast_fusion
  542.1 1.6 slice-done
  543.7 3.0 reshape.280
  546.6 2.5 copy.47
  549.1 0.9 fusion.8
  550.0 1.6 fusion.1
  551.6 0.8 copy.52
  552.3 0.7 broadcast_divide_fusion
  (46 shorter events, 2.5 us)
Async XLA Ops:
  7.2 373.2 %all-reduce.6.cloned.1.call-start = ((), (), s32[]{:S(2)}) async-start(), calls=%async_computation.3 | async-start | bytes 4194304
  11.1 3.0 copy-start
  15.5 2.0 copy-start.1
  23.6 2.1 copy-start.4
  23.6 516.3 %all-gather.4.cloned.1.call-start = ((), (), s32[]{:S(2)}) async-start(), calls=%async_computation.2 | async-start | bytes 3276800 | tf_op jit(solution)/shard_map/all_gather | solution.py:113
  502.5 1.4 copy-start.2
  502.5 6.0 %copy-start.3 = (f32[16,1024]{1,0:T(8,128)S(1)}, f32[16,1024]{1,0:T(8,128)}, u32[]{:S(2)}) copy-start(f32[16,1024]{1,0:T(8,128)} %param.11) | copy-start | bytes 196612
  504.5 8.8 %all-to-all-start.1 = ((f32[16,4,512]{2,0,1:T(8,128)}), f32[16,4,512]{2,0,1:T(8,128)S(1)}, u32[]{:S(2)}, u32[]{:S(2)}) async-start(f32[16,4,512]{2,0,1:T(8,128)} %bitcast.70), calls=%async_computation.1 | async-start | bytes 262144 | tf_op jit(solution)/shard_map/all_to_all | solution.py:117
  542.1 1.6 slice-start
Sparse Core Ops, SparseCore 0:
  23.7 356.6 all-reduce.5
  504.0 35.9 all-gather.3
